TPU v7x, 256 devices: a whole 4x4x8 slice. The times are simulated.
256 devices in a mesh: tok: 32 (over z, y), voc: 8 (over x, core).
Axes of the slice: x: 4, y: 4, z: 8, core: 2. Of those that a mesh axis runs over, the one named last changes fastest.
Arguments:
- hidden: bfloat16 [8192, 1536], P('tok'), may hold values from -1000 to 1000
- norm_gain: float32 [1536], replicated, may hold values from 0.1 to 1.9
- head_weight: bfloat16 [1536, 49152], P(None, ('tok', 'voc')), may hold values from -8 to 8
- targets: int32 [8192], P('tok'), may hold values from 0 to 49151
- lengths: int32 [32], replicated, may hold values from 1 to 256, 5120 in all
- prior_device: int32 [32], replicated, may hold values from 0 to 31, each once
- prior_row: int32 [32], replicated, may hold values from 0 to 255
Outputs:
- logprob: float32 [8192], P('tok')
- entropy: float32 [8192], P('tok')
Inputs may be any that keep to these rules, and one draw needn't show every extreme that they name: One turn's block is full, lengths[t] = 256. `prior_device`: every block index appears once.
All inputs are finite; a program needn't handle non-finite values.
Results may differ from a plain program's by a relative error of at most 0.0036.
Values may be sent and summed in bfloat16 or wider, within the bound.
A program may use at most 192 MiB of HBM per device.

v0:
```python
import jax
import jax.numpy as jnp
from jax import lax
from jax.sharding import PartitionSpec as P

epsilon = 1e-05


def select_entry(table, wanted):
    positions = jnp.arange(table.shape[0], dtype=jnp.int32)
    return jnp.sum(jnp.where(positions == wanted, table, 0))


def combine(first, second):
    largest = jnp.maximum(first[0], second[0])
    later = jnp.exp(second[0] - largest)
    return (largest, second[1] * later, second[2] * later, second[3])


def block_size(total_rows):
    for candidate in (512, 384, 256, 128):
        if total_rows % candidate == 0:
            return candidate
    return total_rows


def block_stats(states, columns, target_col):
    total_rows = states.shape[0]
    block_rows = block_size(total_rows)
    block_count = total_rows // block_rows
    column_ids = jnp.arange(columns.shape[1], dtype=jnp.int32)

    def score_block(inputs):
        state_rows, wanted = inputs
        logits = jnp.dot(state_rows, columns, preferred_element_type=jnp.float32)
        maxima = jnp.max(logits, axis=1)
        weights = jnp.exp(logits - maxima[:, None])
        totals = jnp.sum(weights, axis=1)
        moments = jnp.sum(weights * logits, axis=1)
        picked = jnp.sum(jnp.where(column_ids[None, :] == wanted[:, None], logits, 0.0), axis=1)
        return (maxima, totals, moments, picked)

    results = lax.map(
        score_block,
        (
            states.reshape(block_count, block_rows, states.shape[1]),
            target_col.reshape(block_count, block_rows),
        ),
    )
    return tuple((member.reshape(total_rows) for member in results))


def body(hidden, norm_gain, head_weight, targets, lengths, prior_device, prior_row):
    row_count = hidden.shape[0]
    col_width = head_weight.shape[1]
    tok_index = lax.axis_index("tok")
    band_index = lax.axis_index("voc")
    voc_count = lax.axis_size("voc")
    asked_row = jnp.sum(jnp.where(prior_device == tok_index, prior_row, 0))
    outgoing = lax.dynamic_slice_in_dim(hidden, asked_row, 1, 0)
    incoming = lax.all_gather(outgoing, "tok", axis=0, tiled=True)
    source = select_entry(prior_device, tok_index)
    chosen = jnp.arange(incoming.shape[0], dtype=jnp.int32) == source
    fetched = jnp.sum(
        jnp.where(chosen[:, None], incoming.astype(jnp.float32), 0.0), axis=0, keepdims=True
    )
    scored = jnp.concatenate([fetched, hidden[:-1].astype(jnp.float32)], axis=0)
    normed = (
        scored
        * lax.rsqrt(jnp.mean(scored * scored, axis=1, keepdims=True) + epsilon)
        * norm_gain[None, :]
    ).astype(jnp.bfloat16)
    owner_block = targets // col_width
    target_col = jnp.where(
        owner_block % voc_count == band_index,
        owner_block // voc_count * col_width + targets % col_width,
        -1,
    )
    zeroes = jnp.zeros((row_count,), jnp.float32)
    initial = (jnp.full((row_count,), -1e30, jnp.float32), zeroes, zeroes, zeroes)
    maxima, totals, moments, picked = combine(
        initial,
        block_stats(normed, lax.all_gather(head_weight, "tok", axis=1, tiled=True), target_col),
    )
    largest = lax.pmax(maxima, "voc")
    factor = jnp.exp(maxima - largest)
    totals, moments, picked = lax.psum((totals * factor, moments * factor, picked), "voc")
    maxima = largest
    normalizer = maxima + jnp.log(totals)
    logprob = picked - normalizer
    entropy = normalizer - moments / totals
    live_count = select_entry(lengths, tok_index)
    valid = jnp.arange(row_count, dtype=jnp.int32) < live_count
    return (jnp.where(valid, logprob, 0.0), jnp.where(valid, entropy, 0.0))


def solution(mesh):
    in_specs = (P("tok", None), P(), P(None, ("tok", "voc")), P("tok"), P(), P(), P())
    out_specs = (P("tok"), P("tok"))
    return jax.shard_map(body, mesh=mesh, in_specs=in_specs, out_specs=out_specs, check_vma=False)
```

profile of v0, /device:TPU:1, one launch (start us, length us, event | category | flops | bytes accessed | tf_op | source)
XLA Modules:
  0.0 215.5 jit_solution(13861891363892837926)
XLA Ops:
  7.2 0.0 copy-start
  7.2 0.0 all-gather.3.cloned.1.call-start
  7.2 0.7 all-gather.3.cloned.1.call-update
  7.9 1.3 fusion.7
  11.2 0.8 dynamic-slice_bitcast_fusion
  11.9 42.7 %all-gather = bf16[32,1,1536]{2,1,0:T(2,128)(2,1)S(1)} all-gather(bf16[1,1,1536]{2,1,0:T(2,128)(2,1)S(1)} %dynamic-slice_bitcast_fusion), channel_id=1, replica_groups=mesh['tok'=32,'voc'=8] {'tok'}, dimensions={0}, use_global_device_ids=true | all-gather | bytes 101376 | tf_op jit(solution)/shard_map/all_gather | solution.py:61
  54.6 0.2 convert_element_type.12
  54.8 0.7 iota_compare_fusion.2
  55.5 0.1 fusion.4
  55.6 0.0 copy-done
  55.6 0.0 copy-start.3
  55.6 0.0 copy-start.1
  55.7 0.0 copy-start.2
  55.7 0.2 slice_convert_fusion
  55.8 0.3 multiply_reduce_fusion.1
  56.1 0.1 copy-done.3
  56.3 0.6 fusion.6
  56.9 0.0 copy-done.1
  57.0 108.5 %all-gather.3.cloned.1.call-done = bf16[1536,6144]{0,1:T(8,128)(2,1)} async-done(((bf16[1536,192]{0,1:T(8,128)(2,1)}), bf16[1536,6144]{0,1:T(8,128)(2,1)}) %all-gather.3.cloned.1.call-update) | async-done | bytes 18874384 | tf_op jit(solution)/shard_map/all_gather | solution.py:83
  165.4 10.8 %fusion.10 = (f32[256]{0:T(256)S(1)}, f32[256,6144]{1,0:T(8,128)}) fusion(bf16[1536,6144]{0,1:T(8,128)(2,1)} %all-gather.3.cloned.1.call-done, f32[255,1536]{1,0:T(8,128)S(1)} %slice_convert_fusion, f32[1,1536]{1,0:T(1,128)S(1)} %broadcast_in_dim.57, f32[1536]{0:T(1024)S(1)} %copy-done.2, f32[256]{0:T(256)S(1)} %add_rsqrt_fusion), kind=kOutput, calls=%fused_computation.42 | convolution fusion | flops 4834983936 | bytes 26746880 | tf_op jit(solution)/shard_map/while/body/eval_jaxpr/dot_general | solution.py:35
  176.3 12.8 %pmax.7 = f32[256]{0:T(256)S(1)} all-reduce(f32[256]{0:T(256)S(1)} %broadcast_maximum_fusion), channel_id=1, replica_groups=mesh['tok'=32,'voc'=8] {'voc'}, use_global_device_ids=true, to_apply=%region_8.9 | all-reduce | flops 256 | bytes 2048 | tf_op jit(solution)/shard_map/pmax | solution.py:85
  189.1 4.2 %multiply_reduce_fusion = (f32[256]{0:T(256)S(1)}, f32[256]{0:T(256)S(1)}, f32[256]{0:T(256)S(1)}) fusion(f32[256,6144]{1,0:T(8,128)} %get-tuple-element.42, f32[256]{0:T(256)S(1)} %get-tuple-element.41, s32[256]{0:T(256)S(1)} %compare_select_fusion.1), kind=kLoop, calls=%fused_computation | loop fusion | flops 11009280 | bytes 6296576 | tf_op jit(solution)/shard_map/while/body/eval_jaxpr/reduce_sum | solution.py:39
  193.2 14.2 %all-reduce = (f32[256]{0:T(256)S(1)}, f32[256]{0:T(256)S(1)}, f32[256]{0:T(256)S(1)}) all-reduce(f32[256]{0:T(256)S(1)} %get-tuple-element.22, f32[256]{0:T(256)S(1)} %get-tuple-element.40, f32[256]{0:T(256)S(1)} %get-tuple-element.39), channel_id=1, replica_groups=mesh['tok'=32,'voc'=8] {'voc'}, use_global_device_ids=true, to_apply=%region_6.7 | all-reduce | flops 768 | bytes 6144 | tf_op jit(solution)/shard_map/psum | solution.py:87
  207.4 1.2 subtract_select_fusion
  (6 shorter events, 0.1 us)
Async XLA Ops:
  7.2 48.5 %copy-start = (bf16[256,1536]{1,0:T(8,128)(2,1)S(1)}, bf16[256,1536]{1,0:T(8,128)(2,1)}, u32[]{:S(2)}) copy-start(bf16[256,1536]{1,0:T(8,128)(2,1)} %param.7) | copy-start | bytes 2359300
  7.2 158.2 %all-gather.3.cloned.1.call-start = ((), (), s32[]{:S(2)}) async-start(), calls=%async_computation | async-start | bytes 19464192 | tf_op jit(solution)/shard_map/all_gather | solution.py:83
  55.6 0.7 copy-start.3
  55.6 1.3 copy-start.1
  55.7 109.8 %copy-start.2 = (f32[1536]{0:T(1024)S(1)}, f32[1536]{0:T(1024)}, u32[]{:S(2)}) copy-start(f32[1536]{0:T(1024)} %param.8) | copy-start | bytes 18436
Sparse Core Ops, SparseCore 0:
  10.6 154.7 all-gather.2
where the time goes:
time: 216 us; the launch traced here: 215 us
  waiting for transfers between devices  109 us (50%)
  blocking collectives  69.7 us (32%)
  between operations  16.1 us (7%)
  matrix products  10.8 us (5%)
  other arithmetic  8.77 us (4%)
    all_gather x1, waiting for transfers between devices, body(): lax.all_gather(head_weight, 'tok', axis=1, tiled=True)  108 us
    all_gather x1, blocking collectives, body(): incoming = lax.all_gather(outgoing, 'tok', axis=0, tiled=True)  42.7 us
    psum x1, blocking collectives, body(): lax.psum((totals * factor, moments * factor, picked), 'voc')  14.2 us
    pmax x1, blocking collectives, body(): largest = lax.pmax(maxima, 'voc')  12.8 us
    dot_general x1, matrix products, score_block(): logits = jnp.dot(state_rows, columns, preferred_element_type=jnp.float32)  10.8 us
  transfers between devices with their start and end apart: 1, of which 1 were waited for; matrix products, arithmetic and copies ran while one was open for 2% of the time, Pallas kernels for 0%

commit v1 on v0

--- a/solution.py
+++ b/solution.py
@@ -80,7 +80,13 @@
     initial = (jnp.full((row_count,), -1e30, jnp.float32), zeroes, zeroes, zeroes)
     maxima, totals, moments, picked = combine(
         initial,
-        block_stats(normed, lax.all_gather(head_weight, "tok", axis=1, tiled=True), target_col),
+        block_stats(
+            normed,
+            jnp.concatenate(
+                lax.all_to_all(jnp.stack([head_weight] * lax.axis_size("tok")), "tok", 0, 0), axis=1
+            ),
+            target_col,
+        ),
     )
     largest = lax.pmax(maxima, "voc")
     factor = jnp.exp(maxima - largest)

time: 216 us -> 559 us (2.59)
  blocking collectives: 69.7 us -> 517 us
  waiting for transfers between devices: 109 us -> 0.01 us
  between operations: 16.1 us -> 2.71 us
  starting transfers between devices: 0.04 us -> 12.3 us
  local copies, waits for them, and re-layouts: 0.93 us -> 7.82 us
    all_gather x1, blocking collectives: 42.7 us -> 482 us  [body(): incoming = lax.all_gather(outgoing, 'tok', axis=0, tiled=True)]
    all_gather x1 -> x0, waiting for transfers between devices: 108 us -> none  [body(): lax.all_gather(head_weight, 'tok', axis=1, tiled=True)]
    all_to_all x0 -> x1, starting transfers between devices: none -> 12.3 us  [body(): lax.all_to_all(jnp.stack([head_weight] * lax.axis_size('tok')), 'tok', 0, 0)]
    pmax x1, blocking collectives: 12.8 us -> 22.3 us  [body(): largest = lax.pmax(maxima, 'voc')]
    another operation x0 -> x1, local copies, waits for them, and re-layouts: none -> 7.62 us  [body(): jnp.stack([head_weight] * lax.axis_size('tok'))]
  transfers between devices with their start and end apart: 1 -> 1, of which waited for: 1 -> 0; matrix products, arithmetic and copies ran while one was open for 2% -> 0% of each run, Pallas kernels for 0% -> 0%
where the time goes in v1:
time: 559 us
  blocking collectives  517 us (92%)
  starting transfers between devices  12.3 us (2%)
  matrix products  10.9 us (2%)
  other arithmetic  8.1 us (1%)
  local copies, waits for them, and re-layouts  7.82 us (1%)
    all_gather x1, blocking collectives, body(): incoming = lax.all_gather(outgoing, 'tok', axis=0, tiled=True)  482 us
    pmax x1, blocking collectives, body(): largest = lax.pmax(maxima, 'voc')  22.3 us
    psum x1, blocking collectives, body(): lax.psum((totals * factor, moments * factor, picked), 'voc')  12.4 us
    all_to_all x1, starting transfers between devices, body(): lax.all_to_all(jnp.stack([head_weight] * lax.axis_size('tok')), 'tok', 0, 0)  12.3 us
  transfers between devices with their start and end apart: 1, of which 0 were waited for; matrix products, arithmetic and copies ran while one was open for 0% of the time, Pallas kernels for 0%

profile of v1, /device:TPU:1, one launch (start us, length us, event | category | flops | bytes accessed | tf_op | source)
XLA Modules:
  0.0 558.8 jit_solution(10724298611261157223)
XLA Ops:
  0.6 7.6 %stack.2 = bf16[32,1536,192]{1,2,0:T(8,128)(2,1)} broadcast(bf16[1536,192]{0,1:T(8,128)(2,1)} %param.9), dimensions={1,2} | broadcast | bytes 19464192 | tf_op jit(solution)/shard_map/stack | solution.py:86
  8.3 12.3 %all-to-all-start = ((bf16[32,1536,192]{1,2,0:T(8,128)(2,1)}), bf16[32,1536,192]{1,2,0:T(8,128)(2,1)}, u32[]{:S(2)}, u32[]{:S(2)}) async-start(bf16[32,1536,192]{1,2,0:T(8,128)(2,1)} %stack.2), calls=%async_computation | async-start | bytes 37748736 | tf_op jit(solution)/shard_map/all_to_all | solution.py:86
  20.6 0.0 copy-done.2
  20.6 0.0 copy-done.3
  20.6 0.6 fusion.7
  23.2 0.0 copy-done
  23.2 482.2 %all-gather = bf16[32,1,1536]{2,1,0:T(2,128)(2,1)S(1)} all-gather(bf16[1,1,1536]{2,1,0:T(2,128)(2,1)S(1)} %dynamic-slice_bitcast_fusion), channel_id=1, replica_groups=mesh['tok'=32,'voc'=8] {'tok'}, dimensions={0}, use_global_device_ids=true | all-gather | bytes 101376 | tf_op jit(solution)/shard_map/all_gather | solution.py:61
  505.4 0.2 convert_element_type.12
  505.7 0.7 iota_compare_fusion.2
  506.3 0.1 fusion.4
  506.4 0.0 copy-start.5
  506.4 0.0 copy-start.1
  506.5 0.0 copy-start.4
  506.5 0.2 slice_convert_fusion
  506.7 0.3 multiply_reduce_fusion.1
  506.9 0.1 copy-done.5
  507.1 0.6 fusion.6
  507.7 0.0 copy-done.1
  507.8 0.0 all-to-all-done
  507.8 10.9 %fusion.10 = (f32[256]{0:T(256)S(1)}, f32[256,6144]{1,0:T(8,128)}) fusion(bf16[1536,6144]{0,1:T(8,128)(2,1)} %bitcast.2, f32[255,1536]{1,0:T(8,128)S(1)} %slice_convert_fusion, f32[1,1536]{1,0:T(1,128)S(1)} %broadcast_in_dim.57, f32[1536]{0:T(1024)S(1)} %copy-done.4, f32[256]{0:T(256)S(1)} %add_rsqrt_fusion), kind=kOutput, calls=%fused_computation.42 | convolution fusion | flops 4834983936 | bytes 26746880 | tf_op jit(solution)/shard_map/while/body/eval_jaxpr/dot_general | solution.py:35
  518.7 22.3 %pmax.7 = f32[256]{0:T(256)S(1)} all-reduce(f32[256]{0:T(256)S(1)} %broadcast_maximum_fusion), channel_id=1, replica_groups=mesh['tok'=32,'voc'=8] {'voc'}, use_global_device_ids=true, to_apply=%region_8.9 | all-reduce | flops 256 | bytes 2048 | tf_op jit(solution)/shard_map/pmax | solution.py:91
  541.0 4.2 multiply_reduce_fusion
  545.1 12.4 %all-reduce = (f32[256]{0:T(256)S(1)}, f32[256]{0:T(256)S(1)}, f32[256]{0:T(256)S(1)}) all-reduce(f32[256]{0:T(256)S(1)} %get-tuple-element.22, f32[256]{0:T(256)S(1)} %get-tuple-element.40, f32[256]{0:T(256)S(1)} %get-tuple-element.39), channel_id=1, replica_groups=mesh['tok'=32,'voc'=8] {'voc'}, use_global_device_ids=true, to_apply=%region_6.7 | all-reduce | flops 768 | bytes 6144 | tf_op jit(solution)/shard_map/psum | solution.py:93
  557.6 1.2 subtract_select_fusion
  (10 shorter events, 0.1 us)
Async XLA Ops:
  8.2 12.3 %copy-start.2 = (s32[32]{0:T(128)S(1)}, s32[32]{0:T(128)}, u32[]{:S(2)}) copy-start(s32[32]{0:T(128)} %param.12) | copy-start | bytes 388
  8.3 12.3 %copy-start.3 = (s32[32]{0:T(128)S(1)}, s32[32]{0:T(128)}, u32[]{:S(2)}) copy-start(s32[32]{0:T(128)} %param.13) | copy-start | bytes 388
  8.3 14.9 %copy-start = (bf16[256,1536]{1,0:T(8,128)(2,1)S(1)}, bf16[256,1536]{1,0:T(8,128)(2,1)}, u32[]{:S(2)}) copy-start(bf16[256,1536]{1,0:T(8,128)(2,1)} %param.7) | copy-start | bytes 2359300
  8.3 499.5 %all-to-all-start = ((bf16[32,1536,192]{1,2,0:T(8,128)(2,1)}), bf16[32,1536,192]{1,2,0:T(8,128)(2,1)}, u32[]{:S(2)}, u32[]{:S(2)}) async-start(bf16[32,1536,192]{1,2,0:T(8,128)(2,1)} %stack.2), calls=%async_computation | async-start | bytes 37748736 | tf_op jit(solution)/shard_map/all_to_all | solution.py:86
  506.4 0.7 copy-start.5
  506.4 1.3 copy-start.1
  506.5 1.3 copy-start.4
